TPU v7x, 32 devices: a whole 2x2x4 slice. The times are simulated.
32 devices in a mesh: wide: 8 (over y, x, core), narrow: 4 (over z).
Axes of the slice: x: 2, y: 2, z: 4, core: 2. Of those that a mesh axis runs over, the one named last changes fastest.
Arguments:
- events: bfloat16 [8192, 1024], P('wide'), may hold values from -36 to 36
- lengths: int32 [24], replicated, may hold values from 1 to 2048, 8192 in all
- in_gain: float32 [1024], replicated, may hold values from 0.1 to 1.9
- w_uvqk: bfloat16 [1024, 8, 512], P(None, 'narrow'), may hold values from -2 to 2, as said below
- out_gain: float32 [8, 128], P('narrow'), may hold values from 0.1 to 1.9
- w_out: bfloat16 [8, 128, 1024], P('narrow'), may hold values from -0.25 to 0.25
Outputs:
- layer_out: bfloat16 [8192, 1024], P('wide', 'narrow')
Inputs may be any that keep to these rules, and one draw needn't show every extreme that they name: `w_uvqk`: projection weights.
All inputs are finite; a program needn't handle non-finite values.
Results may differ from a plain program's by a relative error of at most 0.0036.
Values may be sent and summed in bfloat16 or wider, within the bound.
A program may use at most 64 MiB of HBM per device.

v0:
```python
import jax
import jax.numpy as jnp
from jax import lax
from jax.sharding import PartitionSpec as P


def from_behind(value, axis, steps):
    count = lax.axis_size(axis)
    initial, last = (max(0, -steps), min(count, count - steps))
    return lax.ppermute(value, axis, [(source, source + steps) for source in range(initial, last)])


def fetch_relay(pair):
    return from_behind((pair[0], pair[1]), "wide", 1)


def on_device(events, lengths, in_gain, w_uvqk, out_gain, w_out):
    rows_w = events.shape[0]
    heads_local = w_uvqk.shape[1]
    head_size = out_gain.shape[1]
    events_f = events.astype(jnp.float32)
    average = jnp.mean(events_f, axis=-1, keepdims=True)
    variance = jnp.mean((events_f - average) ** 2, axis=-1, keepdims=True)
    normed = ((events_f - average) * lax.rsqrt(variance + 1e-05) * in_gain).astype(jnp.bfloat16)
    projected = jnp.einsum("rd,dhc->rhc", normed, w_uvqk, preferred_element_type=jnp.float32)
    projected = jax.nn.silu(projected).astype(jnp.bfloat16)
    update_gate = projected[:, :, :head_size]
    values_own = projected[:, :, head_size : 2 * head_size]
    queries = projected[:, :, 2 * head_size : 3 * head_size]
    keys_own = projected[:, :, 3 * head_size :]
    user_ends = jnp.cumsum(lengths)

    def owner_of(grow):
        return jnp.sum((user_ends[None, :] <= grow[:, None]).astype(jnp.int32), axis=1)

    first_row = lax.axis_index("wide") * rows_w
    query_pos = first_row + jnp.arange(rows_w, dtype=jnp.int32)
    query_user = owner_of(query_pos)
    scaling = head_size ** (-0.5)

    def attend(running, key_rows, value_rows, key_first):
        key_count = key_rows.shape[0]
        block_rows = 512

        def block_step(carry, block_index):
            key_start = block_index * block_rows
            key_block = lax.dynamic_slice_in_dim(key_rows, key_start, block_rows, 0)
            value_block = lax.dynamic_slice_in_dim(value_rows, key_start, block_rows, 0)
            key_pos = key_first + key_start + jnp.arange(block_rows, dtype=jnp.int32)
            key_user = owner_of(key_pos)
            allowed = (
                (key_user[None, :] == query_user[:, None])
                & (key_pos[None, :] <= query_pos[:, None])
                & (key_pos[None, :] >= 0)
            )
            scores = (
                jnp.einsum("rhc,khc->hrk", queries, key_block, preferred_element_type=jnp.float32)
                * scaling
            )
            weights = jnp.where(allowed[None], jax.nn.silu(scores), 0.0).astype(jnp.bfloat16)
            carry = carry + jnp.einsum(
                "hrk,khc->rhc", weights, value_block, preferred_element_type=jnp.float32
            )
            return (carry, None)

        running, _ = lax.scan(
            block_step, running, jnp.arange(key_count // block_rows, dtype=jnp.int32)
        )
        return running

    attended = attend(
        jnp.zeros((rows_w, heads_local, head_size), jnp.float32), keys_own, values_own, first_row
    )
    reach = lax.axis_size("wide") // 4

    def relay_turn(turn_index, carry):
        keys_held, values_held, running = carry
        keys_held, values_held = fetch_relay((keys_held, values_held))
        running = attend(running, keys_held, values_held, first_row - turn_index * rows_w)
        return (keys_held, values_held, running)

    _, _, attended = lax.fori_loop(1, reach + 1, relay_turn, (keys_own, values_own, attended))
    centre = jnp.mean(attended, axis=-1, keepdims=True)
    deviation = jnp.mean((attended - centre) ** 2, axis=-1, keepdims=True)
    gated = (
        (attended - centre)
        * lax.rsqrt(deviation + 1e-05)
        * out_gain[None]
        * update_gate.astype(jnp.float32)
    )
    gated = gated.astype(jnp.bfloat16)
    columns = lax.all_to_all(w_out, "narrow", split_axis=2, concat_axis=0, tiled=True)
    summed = jnp.einsum(
        "rhc,hcd->rd",
        lax.all_gather(gated, "narrow", axis=1, tiled=True),
        columns,
        preferred_element_type=jnp.float32,
    )
    share = summed.shape[1]
    own_cols = lax.dynamic_slice_in_dim(events_f, lax.axis_index("narrow") * share, share, 1)
    return (own_cols + summed).astype(jnp.bfloat16)


def solution(mesh):
    in_specs = (
        P("wide", None),
        P(),
        P(),
        P(None, "narrow", None),
        P("narrow", None),
        P("narrow", None, None),
    )
    out_specs = P("wide", "narrow")
    return jax.shard_map(
        on_device, mesh=mesh, in_specs=in_specs, out_specs=out_specs, check_vma=False
    )
```

profile of v0, /device:TPU:3, one launch (start us, length us, event | category | flops | bytes accessed | tf_op | source)
XLA Modules:
  0.0 165.2 jit_solution(15008756031488288233)
XLA Ops:
  8.6 2.3 %multiply_reduce_fusion = f32[1024]{0:T(1024)S(1)} fusion(bf16[1024,1024]{1,0:T(8,128)(2,1)} %param.12, f32[1024]{0:T(1024)S(1)} %broadcast_multiply_fusion.1), kind=kLoop, calls=%fused_computation.46 | loop fusion | flops 4193280 | bytes 2105344 | tf_op jit(solution)/shard_map/reduce_sum | solution.py:23
  11.0 3.4 %multiply_convert_fusion = bf16[1024,2,512]{2,0,1:T(8,128)(2,1)S(1)} fusion(bf16[1024,2,512]{2,1,0:T(2,128)(2,1)S(1)} %copy-done, bf16[1024,1024]{1,0:T(8,128)(2,1)S(1)} %copy-done.1, f32[1024]{0:T(1024)S(1)} %copy-done.5, f32[1024]{0:T(1024)S(1)} %add_rsqrt_fusion.1, f32[1024]{0:T(1024)S(1)} %broadcast_multiply_fusion.1), kind=kOutput, calls=%fused_computation.44 | convolution fusion | flops 2157969408 | bytes 6303744 | tf_op jit(solution)/shard_map/rd,dhc->rhc/dot_general | solution.py:25
  17.6 12.9 %while.56 = (s32[]{:T(128)}, f32[1024,2,128]{0,2,1:T(8,128)}, s32[2]{0:T(128)S(1)}, bf16[1024,2,128]{0,2,1:T(8,128)(2,1)S(1)}, s32[24]{0:T(128)S(1)}, /*index=5*...) while((s32[]{:T(128)}, f32[1024,2,128]{0,2,1:T(8,128)}, ...), condition=%wide.region_6.7_spmd.clone.clone.clone, body=%wide.region_4.6_spmd.clone.clone.clone.sunk | while | flops 546871296 | bytes 4219704 | solution.py:66
  19.6 4.2 %fusion.65 = f32[1024,2,128]{0,2,1:T(8,128)} fusion(bf16[1024,2,128]{2,0,1:T(8,128)(2,1)} %get-tuple-element.781, pred[1024,512]{0,1:T(8,128)(4,1)S(1)} %and_and_fusion.4, f32[1024,2,128]{0,2,1:T(8,128)} %get-tuple-element.761, pred[]{:T(512)S(6)} %compare.5, bf16[1024,2,128]{2,0,1:T(8,128)(2,1)} %get-tuple-element.780, s32[]{:T(128)S(6)} %select_n.48, ...), kind=kOutput, calls=%fused_computation.33.clone.1 | convolution fusion | flops 544735232 | bytes 3671552 | tf_op jit(solution)/shard_map/while/body/eval_jaxpr/hrk,khc->rhc/dot_general | solution.py:61
  25.9 4.6 %fusion.65 = f32[1024,2,128]{0,2,1:T(8,128)} fusion(bf16[1024,2,128]{2,0,1:T(8,128)(2,1)} %get-tuple-element.781, pred[1024,512]{0,1:T(8,128)(4,1)S(1)} %and_and_fusion.4, f32[1024,2,128]{0,2,1:T(8,128)} %get-tuple-element.761, pred[]{:T(512)S(6)} %compare.5, bf16[1024,2,128]{2,0,1:T(8,128)(2,1)} %get-tuple-element.780, s32[]{:T(128)S(6)} %select_n.48, ...), kind=kOutput, calls=%fused_computation.33.clone.1 | convolution fusion | flops 544735232 | bytes 3671552 | tf_op jit(solution)/shard_map/while/body/eval_jaxpr/hrk,khc->rhc/dot_general | solution.py:61
  30.5 62.6 %while.55 = (s32[]{:T(128)}, bf16[1024,2,128]{2,0,1:T(8,128)(2,1)}, bf16[1024,2,128]{0,2,1:T(8,128)(2,1)S(1)}, f32[1024,2,128]{0,2,1:T(8,128)}, s32[]{:T(128)}, ...) while((s32[]{:T(128)}, bf16[1024,2,128]{2,0,1:T(8,128)(2,1)}, ...), condition=%wide.region_11.12_spmd.clone.clone, body=%wide.region_7.11_spmd.clone.clone.sunk | while | flops 546609152 | bytes 10511020 | solution.py:82
  30.5 3.7 %collective-permute-start = (bf16[1024,2,128]{2,0,1:T(8,128)(2,1)}, bf16[1024,2,128]{2,0,1:T(8,128)(2,1)S(1)}, u32[]{:S(2)}, u32[]{:S(2)}) collective-permute-start(bf16[1024,2,128]{2,0,1:T(8,128)(2,1)} %get-tuple-element.802), channel_id=1, source_target_pairs={{0,4},{4,8},{8,12},{12,16},{16,20},{20,24},{24,28},{1,5},{5,9},{9,... | collective-permute-start | bytes 1572872 | tf_op jit(solution)/shard_map/while/body/eval_jaxpr/ppermute | solution.py:10
  36.1 4.5 %collective-permute-done = bf16[1024,2,128]{2,0,1:T(8,128)(2,1)S(1)} collective-permute-done((bf16[1024,2,128]{2,0,1:T(8,128)(2,1)}, bf16[1024,2,128]{2,0,1:T(8,128)(2,1)S(1)}, u32[]{:S(2)}, u32[]{:S(2)}) %collective-permute-start) | collective-permute-done | bytes 524320 | tf_op jit(solution)/shard_map/while/body/eval_jaxpr/ppermute | solution.py:10
  40.6 5.5 %collective-permute-done.1 = bf16[1024,2,128]{0,2,1:T(8,128)(2,1)} collective-permute-done((bf16[1024,2,128]{0,2,1:T(8,128)(2,1)S(1)}, bf16[1024,2,128]{0,2,1:T(8,128)(2,1)}, u32[]{:S(2)}, u32[]{:S(2)}) %collective-permute-start.1) | collective-permute-done | bytes 524320 | tf_op jit(solution)/shard_map/while/body/eval_jaxpr/ppermute | solution.py:10
  46.1 13.0 %while.57 = (s32[]{:T(128)}, f32[1024,2,128]{0,2,1:T(8,128)}, s32[2]{0:T(128)S(1)}, bf16[1024,2,128]{0,2,1:T(8,128)(2,1)}, s32[24]{0:T(128)S(1)}, /*index=5*/s32...) while((s32[]{:T(128)}, f32[1024,2,128]{0,2,1:T(8,128)}, ...), condition=%wide.region_10.10_spmd, body=%wide.region_8.9_spmd.sunk | while | flops 546608128 | bytes 4215091 | solution.py:66
  48.0 4.6 %fusion.69 = f32[1024,2,128]{0,2,1:T(8,128)} fusion(f32[1024,2,128]{0,2,1:T(8,128)} %get-tuple-element.720, bf16[1024,2,128]{2,0,1:T(8,128)(2,1)} %get-tuple-element.742, pred[1024,512]{0,1:T(8,128)(4,1)S(1)} %and_and_fusion.5, bf16[1024,2,128]{2,0,1:T(8,128)(2,1)S(1)} %get-tuple-element.741, s32[]{:T(128)S(6)} %select_n.50, ...), kind=kOutput, calls=%fused_computation.12.clone.1 | convolution fusion | flops 544473088 | bytes 3671040 | tf_op jit(solution)/shard_map/while/body/eval_jaxpr/while/body/eval_jaxpr/hrk,khc->rhc/dot_general | solution.py:61
  54.5 4.6 %fusion.69 = f32[1024,2,128]{0,2,1:T(8,128)} fusion(f32[1024,2,128]{0,2,1:T(8,128)} %get-tuple-element.720, bf16[1024,2,128]{2,0,1:T(8,128)(2,1)} %get-tuple-element.742, pred[1024,512]{0,1:T(8,128)(4,1)S(1)} %and_and_fusion.5, bf16[1024,2,128]{2,0,1:T(8,128)(2,1)S(1)} %get-tuple-element.741, s32[]{:T(128)S(6)} %select_n.50, ...), kind=kOutput, calls=%fused_computation.12.clone.1 | convolution fusion | flops 544473088 | bytes 3671040 | tf_op jit(solution)/shard_map/while/body/eval_jaxpr/while/body/eval_jaxpr/hrk,khc->rhc/dot_general | solution.py:61
  60.9 5.4 %collective-permute-start = (bf16[1024,2,128]{2,0,1:T(8,128)(2,1)}, bf16[1024,2,128]{2,0,1:T(8,128)(2,1)S(1)}, u32[]{:S(2)}, u32[]{:S(2)}) collective-permute-start(bf16[1024,2,128]{2,0,1:T(8,128)(2,1)} %get-tuple-element.802), channel_id=1, source_target_pairs={{0,4},{4,8},{8,12},{12,16},{16,20},{20,24},{24,28},{1,5},{5,9},{9,... | collective-permute-start | bytes 1572872 | tf_op jit(solution)/shard_map/while/body/eval_jaxpr/ppermute | solution.py:10
  68.3 4.5 %collective-permute-done = bf16[1024,2,128]{2,0,1:T(8,128)(2,1)S(1)} collective-permute-done((bf16[1024,2,128]{2,0,1:T(8,128)(2,1)}, bf16[1024,2,128]{2,0,1:T(8,128)(2,1)S(1)}, u32[]{:S(2)}, u32[]{:S(2)}) %collective-permute-start) | collective-permute-done | bytes 524320 | tf_op jit(solution)/shard_map/while/body/eval_jaxpr/ppermute | solution.py:10
  72.7 5.5 %collective-permute-done.1 = bf16[1024,2,128]{0,2,1:T(8,128)(2,1)} collective-permute-done((bf16[1024,2,128]{0,2,1:T(8,128)(2,1)S(1)}, bf16[1024,2,128]{0,2,1:T(8,128)(2,1)}, u32[]{:S(2)}, u32[]{:S(2)}) %collective-permute-start.1) | collective-permute-done | bytes 524320 | tf_op jit(solution)/shard_map/while/body/eval_jaxpr/ppermute | solution.py:10
  78.3 13.0 %while.57 = (s32[]{:T(128)}, f32[1024,2,128]{0,2,1:T(8,128)}, s32[2]{0:T(128)S(1)}, bf16[1024,2,128]{0,2,1:T(8,128)(2,1)}, s32[24]{0:T(128)S(1)}, /*index=5*/s32...) while((s32[]{:T(128)}, f32[1024,2,128]{0,2,1:T(8,128)}, ...), condition=%wide.region_10.10_spmd, body=%wide.region_8.9_spmd.sunk | while | flops 546608128 | bytes 4215091 | solution.py:66
  80.2 4.6 %fusion.69 = f32[1024,2,128]{0,2,1:T(8,128)} fusion(f32[1024,2,128]{0,2,1:T(8,128)} %get-tuple-element.720, bf16[1024,2,128]{2,0,1:T(8,128)(2,1)} %get-tuple-element.742, pred[1024,512]{0,1:T(8,128)(4,1)S(1)} %and_and_fusion.5, bf16[1024,2,128]{2,0,1:T(8,128)(2,1)S(1)} %get-tuple-element.741, s32[]{:T(128)S(6)} %select_n.50, ...), kind=kOutput, calls=%fused_computation.12.clone.1 | convolution fusion | flops 544473088 | bytes 3671040 | tf_op jit(solution)/shard_map/while/body/eval_jaxpr/while/body/eval_jaxpr/hrk,khc->rhc/dot_general | solution.py:61
  86.7 4.6 %fusion.69 = f32[1024,2,128]{0,2,1:T(8,128)} fusion(f32[1024,2,128]{0,2,1:T(8,128)} %get-tuple-element.720, bf16[1024,2,128]{2,0,1:T(8,128)(2,1)} %get-tuple-element.742, pred[1024,512]{0,1:T(8,128)(4,1)S(1)} %and_and_fusion.5, bf16[1024,2,128]{2,0,1:T(8,128)(2,1)S(1)} %get-tuple-element.741, s32[]{:T(128)S(6)} %select_n.50, ...), kind=kOutput, calls=%fused_computation.12.clone.1 | convolution fusion | flops 544473088 | bytes 3671040 | tf_op jit(solution)/shard_map/while/body/eval_jaxpr/while/body/eval_jaxpr/hrk,khc->rhc/dot_general | solution.py:61
  96.7 2.4 %multiply_convert_fusion.2 = bf16[1024,2,128]{2,0,1:T(8,128)(2,1)} fusion(f32[1024,2,128]{2,0,1:T(8,128)S(1)} %copy.38, bf16[1024,2,512]{2,0,1:T(8,128)(2,1)} %copy-done.2, f32[2,128]{1,0:T(2,128)S(1)} %copy-done.3, f32[1024,2]{0,1:T(2,128)S(1)} %add_rsqrt_fusion, f32[1024,2]{0,1:T(2,128)S(1)} %broadcast_multiply_fusion), kind=kLoop, calls=%fused_computation.57 | loop fusion | flops 1572864 | bytes 2114560 | tf_op jit(solution)/shard_map/convert_element_type | solution.py:91
  101.1 4.6 %all-to-all-start = ((bf16[2,128,1024]{1,0,2:T(2,128)(2,1)}), bf16[2,128,1024]{1,0,2:T(2,128)(2,1)S(1)}, u32[]{:S(2)}, u32[]{:S(2)}) async-start(bf16[2,128,1024]{1,0,2:T(2,128)(2,1)} %copy.39), calls=%async_computation | async-start | bytes 1048576 | tf_op jit(solution)/shard_map/all_to_all | solution.py:92
  105.7 4.0 %convert_element_type.33 = f32[1024,1024]{1,0:T(8,128)} convert(bf16[1024,1024]{1,0:T(8,128)(2,1)} %param.12) | non-fusion elementwise | flops 1048576 | bytes 6291456 | tf_op jit(solution)/shard_map/convert_element_type | solution.py:21
  109.6 17.5 %all-to-all-done = bf16[2,128,1024]{1,0,2:T(2,128)(2,1)S(1)} async-done(((bf16[2,128,1024]{1,0,2:T(2,128)(2,1)}), bf16[2,128,1024]{1,0,2:T(2,128)(2,1)S(1)}, u32[]{:S(2)}, u32[]{:S(2)}) %all-to-all-start) | async-done | bytes 524320 | tf_op jit(solution)/shard_map/all_to_all | solution.py:92
  127.5 27.4 %all-gather.2.cloned.1.call-done = bf16[1024,8,128]{2,0,1:T(8,128)(2,1)} async-done(((bf16[1024,2,128]{2,0,1:T(8,128)(2,1)}), bf16[1024,8,128]{2,0,1:T(8,128)(2,1)}) %all-gather.2.cloned.1.call-update) | async-done | bytes 2097168 | tf_op jit(solution)/shard_map/all_gather | solution.py:95
  154.9 3.4 %fusion.48 = bf16[1024,256]{1,0:T(8,128)(2,1)} fusion(bf16[1024,8,128]{2,0,1:T(8,128)(2,1)} %all-gather.2.cloned.1.call-done, bf16[8,128,256]{2,1,0:T(8,128)(2,1)S(1)} %bitcast.89, f32[1024,1024]{1,0:T(8,128)} %convert_element_type.33, s32[]{:T(128)S(6)} %select_n.18), kind=kOutput, calls=%fused_computation.56 | convolution fusion | flops 537395200 | bytes 4194308 | tf_op jit(solution)/shard_map/rhc,hcd->rd/dot_general | solution.py:93
  (75 shorter events, 26.3 us)
Async XLA Ops:
  6.5 4.4 %copy-start = (bf16[1024,2,512]{2,1,0:T(2,128)(2,1)S(1)}, bf16[1024,2,512]{2,1,0:T(2,128)(2,1)}, u32[]{:S(2)}) copy-start(bf16[1024,2,512]{2,1,0:T(2,128)(2,1)} %param.15) | copy-start | bytes 6291460
  6.5 4.4 %copy-start.5 = (f32[1024]{0:T(1024)S(1)}, f32[1024]{0:T(1024)}, u32[]{:S(2)}) copy-start(f32[1024]{0:T(1024)} %param.14) | copy-start | bytes 12292
  6.5 148.4 %all-gather.2.cloned.1.call-start = ((), (), s32[]{:S(2)}) async-start(), calls=%async_computation.1 | async-start | bytes 2621440 | tf_op jit(solution)/shard_map/all_gather | solution.py:95
  6.5 4.4 %copy-start.1 = (bf16[1024,1024]{1,0:T(8,128)(2,1)S(1)}, bf16[1024,1024]{1,0:T(8,128)(2,1)}, u32[]{:S(2)}) copy-start(bf16[1024,1024]{1,0:T(8,128)(2,1)} %param.12) | copy-start | bytes 6291460
  14.4 1.4 copy-start.2
  15.7 1.5 copy-start.4
  30.5 10.1 %collective-permute-start = (bf16[1024,2,128]{2,0,1:T(8,128)(2,1)}, bf16[1024,2,128]{2,0,1:T(8,128)(2,1)S(1)}, u32[]{:S(2)}, u32[]{:S(2)}) collective-permute-start(bf16[1024,2,128]{2,0,1:T(8,128)(2,1)} %get-tuple-element.802), channel_id=1, source_target_pairs={{0,4},{4,8},{8,12},{12,16},{16,20},{20,24},{24,28},{1,5},{5,9},{9,... | collective-permute-start | bytes 1572872 | tf_op jit(solution)/shard_map/while/body/eval_jaxpr/ppermute | solution.py:10
  34.2 11.9 %collective-permute-start.1 = (bf16[1024,2,128]{0,2,1:T(8,128)(2,1)S(1)}, bf16[1024,2,128]{0,2,1:T(8,128)(2,1)}, u32[]{:S(2)}, u32[]{:S(2)}) collective-permute-start(bf16[1024,2,128]{0,2,1:T(8,128)(2,1)S(1)} %get-tuple-element.803), channel_id=1, source_target_pairs={{0,4},{4,8},{8,12},{12,16},{16,20},{20,24},{24,28},{1,5},{5,9},{9,... | collective-permute-start | bytes 1572872 | tf_op jit(solution)/shard_map/while/body/eval_jaxpr/ppermute | solution.py:10
  60.9 11.8 %collective-permute-start = (bf16[1024,2,128]{2,0,1:T(8,128)(2,1)}, bf16[1024,2,128]{2,0,1:T(8,128)(2,1)S(1)}, u32[]{:S(2)}, u32[]{:S(2)}) collective-permute-start(bf16[1024,2,128]{2,0,1:T(8,128)(2,1)} %get-tuple-element.802), channel_id=1, source_target_pairs={{0,4},{4,8},{8,12},{12,16},{16,20},{20,24},{24,28},{1,5},{5,9},{9,... | collective-permute-start | bytes 1572872 | tf_op jit(solution)/shard_map/while/body/eval_jaxpr/ppermute | solution.py:10
  66.3 11.9 %collective-permute-start.1 = (bf16[1024,2,128]{0,2,1:T(8,128)(2,1)S(1)}, bf16[1024,2,128]{0,2,1:T(8,128)(2,1)}, u32[]{:S(2)}, u32[]{:S(2)}) collective-permute-start(bf16[1024,2,128]{0,2,1:T(8,128)(2,1)S(1)} %get-tuple-element.803), channel_id=1, source_target_pairs={{0,4},{4,8},{8,12},{12,16},{16,20},{20,24},{24,28},{1,5},{5,9},{9,... | collective-permute-start | bytes 1572872 | tf_op jit(solution)/shard_map/while/body/eval_jaxpr/ppermute | solution.py:10
  93.1 3.6 %copy-start.3 = (f32[2,128]{1,0:T(2,128)S(1)}, f32[2,128]{1,0:T(2,128)}, u32[]{:S(2)}) copy-start(f32[2,128]{1,0:T(2,128)} %param.16) | copy-start | bytes 3076
  101.1 26.1 %all-to-all-start = ((bf16[2,128,1024]{1,0,2:T(2,128)(2,1)}), bf16[2,128,1024]{1,0,2:T(2,128)(2,1)S(1)}, u32[]{:S(2)}, u32[]{:S(2)}) async-start(bf16[2,128,1024]{1,0,2:T(2,128)(2,1)} %copy.39), calls=%async_computation | async-start | bytes 1048576 | tf_op jit(solution)/shard_map/all_to_all | solution.py:92
Sparse Core Ops, SparseCore 0:
  99.2 55.7 all-gather.1
where the time goes:
time: 166 us; the launch traced here: 165 us
  waiting for transfers between devices  64.9 us (39%)
  matrix products  33.8 us (20%)
  starting transfers between devices  17.5 us (11%)
  other arithmetic  16.9 us (10%)
  local copies, waits for them, and re-layouts  14.2 us (9%)
  between operations  13.5 us (8%)
  loops' own time  4.27 us (3%)
    all_gather x1, waiting for transfers between devices, on_device(): lax.all_gather(gated, 'narrow', axis=1, tiled=True)  27.4 us
    dot_general x6, matrix products, block_step(): jnp.einsum('hrk,khc->rhc', weights, value_block, preferred_element_type=j...  27.1 us
    ppermute x4, waiting for transfers between devices, from_behind(): lax.ppermute(value, axis, [(source, source + steps) for source in range(i...  20 us
    all_to_all x1, waiting for transfers between devices, on_device(): lax.all_to_all(w_out, 'narrow', split_axis=2, concat_axis=0, tiled=True)  17.5 us
    ppermute x4, starting transfers between devices, from_behind(): lax.ppermute(value, axis, [(source, source + steps) for source in range(i...  12.9 us
    all_to_all x1, starting transfers between devices, on_device(): lax.all_to_all(w_out, 'narrow', split_axis=2, concat_axis=0, tiled=True)  4.59 us
    another operation x3, loops' own time, attend(): lax.scan(block_step, running, jnp.arange(key_count // block_rows, dtype=j...  4.21 us
    convert_element_type x1, other arithmetic, on_device(): events_f = events.astype(jnp.float32)  3.98 us
  transfers between devices with their start and end apart: 6, of which 6 were waited for; matrix products, arithmetic and copies ran while one was open for 4% of the time, Pallas kernels for 0%

commit v1 on v0

--- a/solution.py
+++ b/solution.py
@@ -2,6 +2,27 @@
 import jax.numpy as jnp
 from jax import lax
 from jax.sharding import PartitionSpec as P
+
+
+def joined_along(blocks, dim):
+    dims = list(blocks.shape[1:])
+    dims[dim] *= blocks.shape[0]
+    return jnp.moveaxis(blocks, 0, dim).reshape(dims)
+
+
+def collected_by_bits(x, axis):
+    devices, index = (lax.axis_size(axis), lax.axis_index(axis))
+    blocks, apart = (x[None], 1)
+    while apart < devices:
+        other = lax.ppermute(blocks, axis, [(i, i ^ apart) for i in range(devices)])
+        low = index & apart == 0
+        blocks = jnp.concatenate([jnp.where(low, blocks, other), jnp.where(low, other, blocks)])
+        apart *= 2
+    return blocks
+
+
+def gather_by_bits(value, axis, dim):
+    return joined_along(collected_by_bits(value, axis), dim)
 
 
 def from_behind(value, axis, steps):
@@ -92,7 +113,7 @@
     columns = lax.all_to_all(w_out, "narrow", split_axis=2, concat_axis=0, tiled=True)
     summed = jnp.einsum(
         "rhc,hcd->rd",
-        lax.all_gather(gated, "narrow", axis=1, tiled=True),
+        gather_by_bits(gated, "narrow", 1),
         columns,
         preferred_element_type=jnp.float32,
     )

time: 166 us -> 175 us (1.054)
  waiting for transfers between devices: 64.9 us -> 78.4 us
  between operations: 13.5 us -> 0.18 us
  other arithmetic: 16.9 us -> 21 us
  starting transfers between devices: 17.5 us -> 20.6 us
    all_to_all x1, waiting for transfers between devices: 17.5 us -> 46.6 us  [on_device(): lax.all_to_all(w_out, 'narrow', split_axis=2, concat_axis=0, tiled=True)]
    all_gather x1 -> x0, waiting for transfers between devices: 27.4 us -> none  [on_device(): lax.all_gather(gated, 'narrow', axis=1, tiled=True)]
    ppermute x0 -> x2, waiting for transfers between devices: none -> 11.9 us  [collected_by_bits(): other = lax.ppermute(blocks, axis, [(i, i ^ apart) for i in range(devices)])]
    ppermute x0 -> x2, starting transfers between devices: none -> 3.6 us  [collected_by_bits(): other = lax.ppermute(blocks, axis, [(i, i ^ apart) for i in range(devices)])]
    select_n x0 -> x2, other arithmetic: none -> 2.83 us  [collected_by_bits(): jnp.where(low, blocks, other)]
    broadcast_in_dim x0 -> x1, other arithmetic: none -> 2.36 us  [collected_by_bits(): blocks, apart = (x[None], 1)]
    convert_element_type x1 -> x0, other arithmetic: 2.36 us -> none  [on_device(): gated = gated.astype(jnp.bfloat16)]
    unnamed x14 -> x16, local copies, waits for them, and re-layouts: 3.58 us -> 3.6 us
  transfers between devices with their start and end apart: 6 -> 7, of which waited for: 6 -> 6; matrix products, arithmetic and copies ran while one was open for 4% -> 5% of each run, Pallas kernels for 0% -> 0%
where the time goes in v1:
time: 175 us; the launch traced here: 174 us
  waiting for transfers between devices  78.4 us (45%)
  matrix products  33.2 us (19%)
  other arithmetic  21 us (12%)
  starting transfers between devices  20.6 us (12%)
  local copies, waits for them, and re-layouts  15.8 us (9%)
  loops' own time  4.27 us (2%)
    all_to_all x1, waiting for transfers between devices, on_device(): lax.all_to_all(w_out, 'narrow', split_axis=2, concat_axis=0, tiled=True)  46.6 us
    dot_general x6, matrix products, block_step(): jnp.einsum('hrk,khc->rhc', weights, value_block, preferred_element_type=j...  27.1 us
    ppermute x4, waiting for transfers between devices, from_behind(): lax.ppermute(value, axis, [(source, source + steps) for source in range(i...  20 us
    ppermute x4, starting transfers between devices, from_behind(): lax.ppermute(value, axis, [(source, source + steps) for source in range(i...  12.9 us
    ppermute x2, waiting for transfers between devices, collected_by_bits(): other = lax.ppermute(blocks, axis, [(i, i ^ apart) for i in range(devices)])  11.9 us
    another operation x3, loops' own time, attend(): lax.scan(block_step, running, jnp.arange(key_count // block_rows, dtype=j...  4.21 us
    all_to_all x1, starting transfers between devices, on_device(): lax.all_to_all(w_out, 'narrow', split_axis=2, concat_axis=0, tiled=True)  4.13 us
    convert_element_type x1, other arithmetic, on_device(): events_f = events.astype(jnp.float32)  3.98 us
  transfers between devices with their start and end apart: 7, of which 6 were waited for; matrix products, arithmetic and copies ran while one was open for 5% of the time, Pallas kernels for 0%

profile of v1, /device:TPU:3, one launch (start us, length us, event | category | flops | bytes accessed | tf_op | source)
XLA Modules:
  0.0 173.5 jit_solution(4792431687881772204)
XLA Ops:
  4.4 3.4 %multiply_convert_fusion = bf16[1024,2,512]{2,0,1:T(8,128)(2,1)S(1)} fusion(bf16[1024,2,512]{2,1,0:T(2,128)(2,1)S(1)} %copy-done, bf16[1024,1024]{1,0:T(8,128)(2,1)S(1)} %copy-done.1, f32[1024]{0:T(1024)S(1)} %copy-done.6, f32[1024]{0:T(1024)S(1)} %add_rsqrt_fusion.1, f32[1024]{0:T(1024)S(1)} %broadcast_multiply_fusion.1), kind=kOutput, calls=%fused_computation.44 | convolution fusion | flops 2157969408 | bytes 6303744 | tf_op jit(solution)/shard_map/rd,dhc->rhc/dot_general | solution.py:46
  11.1 12.9 %while.56 = (s32[]{:T(128)}, f32[1024,2,128]{0,2,1:T(8,128)}, s32[2]{0:T(128)S(1)}, bf16[1024,2,128]{0,2,1:T(8,128)(2,1)S(1)}, s32[24]{0:T(128)S(1)}, /*index=5*...) while((s32[]{:T(128)}, f32[1024,2,128]{0,2,1:T(8,128)}, ...), condition=%wide.region_6.7_spmd.clone.clone.clone, body=%wide.region_4.6_spmd.clone.clone.clone.sunk | while | flops 546871296 | bytes 4219704 | solution.py:87
  13.1 4.2 %fusion.66 = f32[1024,2,128]{0,2,1:T(8,128)} fusion(bf16[1024,2,128]{2,0,1:T(8,128)(2,1)} %get-tuple-element.785, pred[1024,512]{0,1:T(8,128)(4,1)S(1)} %and_and_fusion.4, f32[1024,2,128]{0,2,1:T(8,128)} %get-tuple-element.765, pred[]{:T(512)S(6)} %compare.5, bf16[1024,2,128]{2,0,1:T(8,128)(2,1)} %get-tuple-element.784, s32[]{:T(128)S(6)} %select_n.86, ...), kind=kOutput, calls=%fused_computation.33.clone.1 | convolution fusion | flops 544735232 | bytes 3671552 | tf_op jit(solution)/shard_map/while/body/eval_jaxpr/hrk,khc->rhc/dot_general | solution.py:82
  19.4 4.6 %fusion.66 = f32[1024,2,128]{0,2,1:T(8,128)} fusion(bf16[1024,2,128]{2,0,1:T(8,128)(2,1)} %get-tuple-element.785, pred[1024,512]{0,1:T(8,128)(4,1)S(1)} %and_and_fusion.4, f32[1024,2,128]{0,2,1:T(8,128)} %get-tuple-element.765, pred[]{:T(512)S(6)} %compare.5, bf16[1024,2,128]{2,0,1:T(8,128)(2,1)} %get-tuple-element.784, s32[]{:T(128)S(6)} %select_n.86, ...), kind=kOutput, calls=%fused_computation.33.clone.1 | convolution fusion | flops 544735232 | bytes 3671552 | tf_op jit(solution)/shard_map/while/body/eval_jaxpr/hrk,khc->rhc/dot_general | solution.py:82
  24.0 62.6 %while.55 = (s32[]{:T(128)}, bf16[1024,2,128]{2,0,1:T(8,128)(2,1)}, bf16[1024,2,128]{0,2,1:T(8,128)(2,1)S(1)}, f32[1024,2,128]{0,2,1:T(8,128)}, s32[]{:T(128)}, ...) while((s32[]{:T(128)}, bf16[1024,2,128]{2,0,1:T(8,128)(2,1)}, ...), condition=%wide.region_11.12_spmd.clone.clone, body=%wide.region_7.11_spmd.clone.clone.sunk | while | flops 546609152 | bytes 10511020 | solution.py:103
  24.0 3.7 %collective-permute-start = (bf16[1024,2,128]{2,0,1:T(8,128)(2,1)}, bf16[1024,2,128]{2,0,1:T(8,128)(2,1)S(1)}, u32[]{:S(2)}, u32[]{:S(2)}) collective-permute-start(bf16[1024,2,128]{2,0,1:T(8,128)(2,1)} %get-tuple-element.806), channel_id=1, source_target_pairs={{0,4},{4,8},{8,12},{12,16},{16,20},{20,24},{24,28},{1,5},{5,9},{9,... | collective-permute-start | bytes 1572872 | tf_op jit(solution)/shard_map/while/body/eval_jaxpr/ppermute | solution.py:31
  29.6 4.5 %collective-permute-done = bf16[1024,2,128]{2,0,1:T(8,128)(2,1)S(1)} collective-permute-done((bf16[1024,2,128]{2,0,1:T(8,128)(2,1)}, bf16[1024,2,128]{2,0,1:T(8,128)(2,1)S(1)}, u32[]{:S(2)}, u32[]{:S(2)}) %collective-permute-start) | collective-permute-done | bytes 524320 | tf_op jit(solution)/shard_map/while/body/eval_jaxpr/ppermute | solution.py:31
  34.1 5.5 %collective-permute-done.1 = bf16[1024,2,128]{0,2,1:T(8,128)(2,1)} collective-permute-done((bf16[1024,2,128]{0,2,1:T(8,128)(2,1)S(1)}, bf16[1024,2,128]{0,2,1:T(8,128)(2,1)}, u32[]{:S(2)}, u32[]{:S(2)}) %collective-permute-start.1) | collective-permute-done | bytes 524320 | tf_op jit(solution)/shard_map/while/body/eval_jaxpr/ppermute | solution.py:31
  39.6 13.0 %while.57 = (s32[]{:T(128)}, f32[1024,2,128]{0,2,1:T(8,128)}, s32[2]{0:T(128)S(1)}, bf16[1024,2,128]{0,2,1:T(8,128)(2,1)}, s32[24]{0:T(128)S(1)}, /*index=5*/s32...) while((s32[]{:T(128)}, f32[1024,2,128]{0,2,1:T(8,128)}, ...), condition=%wide.region_10.10_spmd, body=%wide.region_8.9_spmd.sunk | while | flops 546608128 | bytes 4215091 | solution.py:87
  41.5 4.6 %fusion.70 = f32[1024,2,128]{0,2,1:T(8,128)} fusion(f32[1024,2,128]{0,2,1:T(8,128)} %get-tuple-element.724, bf16[1024,2,128]{2,0,1:T(8,128)(2,1)} %get-tuple-element.746, pred[1024,512]{0,1:T(8,128)(4,1)S(1)} %and_and_fusion.5, bf16[1024,2,128]{2,0,1:T(8,128)(2,1)S(1)} %get-tuple-element.745, s32[]{:T(128)S(6)} %select_n.88, ...), kind=kOutput, calls=%fused_computation.12.clone.1 | convolution fusion | flops 544473088 | bytes 3671040 | tf_op jit(solution)/shard_map/while/body/eval_jaxpr/while/body/eval_jaxpr/hrk,khc->rhc/dot_general | solution.py:82
  48.0 4.6 %fusion.70 = f32[1024,2,128]{0,2,1:T(8,128)} fusion(f32[1024,2,128]{0,2,1:T(8,128)} %get-tuple-element.724, bf16[1024,2,128]{2,0,1:T(8,128)(2,1)} %get-tuple-element.746, pred[1024,512]{0,1:T(8,128)(4,1)S(1)} %and_and_fusion.5, bf16[1024,2,128]{2,0,1:T(8,128)(2,1)S(1)} %get-tuple-element.745, s32[]{:T(128)S(6)} %select_n.88, ...), kind=kOutput, calls=%fused_computation.12.clone.1 | convolution fusion | flops 544473088 | bytes 3671040 | tf_op jit(solution)/shard_map/while/body/eval_jaxpr/while/body/eval_jaxpr/hrk,khc->rhc/dot_general | solution.py:82
  54.4 5.4 %collective-permute-start = (bf16[1024,2,128]{2,0,1:T(8,128)(2,1)}, bf16[1024,2,128]{2,0,1:T(8,128)(2,1)S(1)}, u32[]{:S(2)}, u32[]{:S(2)}) collective-permute-start(bf16[1024,2,128]{2,0,1:T(8,128)(2,1)} %get-tuple-element.806), channel_id=1, source_target_pairs={{0,4},{4,8},{8,12},{12,16},{16,20},{20,24},{24,28},{1,5},{5,9},{9,... | collective-permute-start | bytes 1572872 | tf_op jit(solution)/shard_map/while/body/eval_jaxpr/ppermute | solution.py:31
  61.8 4.5 %collective-permute-done = bf16[1024,2,128]{2,0,1:T(8,128)(2,1)S(1)} collective-permute-done((bf16[1024,2,128]{2,0,1:T(8,128)(2,1)}, bf16[1024,2,128]{2,0,1:T(8,128)(2,1)S(1)}, u32[]{:S(2)}, u32[]{:S(2)}) %collective-permute-start) | collective-permute-done | bytes 524320 | tf_op jit(solution)/shard_map/while/body/eval_jaxpr/ppermute | solution.py:31
  66.2 5.5 %collective-permute-done.1 = bf16[1024,2,128]{0,2,1:T(8,128)(2,1)} collective-permute-done((bf16[1024,2,128]{0,2,1:T(8,128)(2,1)S(1)}, bf16[1024,2,128]{0,2,1:T(8,128)(2,1)}, u32[]{:S(2)}, u32[]{:S(2)}) %collective-permute-start.1) | collective-permute-done | bytes 524320 | tf_op jit(solution)/shard_map/while/body/eval_jaxpr/ppermute | solution.py:31
  71.8 13.0 %while.57 = (s32[]{:T(128)}, f32[1024,2,128]{0,2,1:T(8,128)}, s32[2]{0:T(128)S(1)}, bf16[1024,2,128]{0,2,1:T(8,128)(2,1)}, s32[24]{0:T(128)S(1)}, /*index=5*/s32...) while((s32[]{:T(128)}, f32[1024,2,128]{0,2,1:T(8,128)}, ...), condition=%wide.region_10.10_spmd, body=%wide.region_8.9_spmd.sunk | while | flops 546608128 | bytes 4215091 | solution.py:87
  73.7 4.6 %fusion.70 = f32[1024,2,128]{0,2,1:T(8,128)} fusion(f32[1024,2,128]{0,2,1:T(8,128)} %get-tuple-element.724, bf16[1024,2,128]{2,0,1:T(8,128)(2,1)} %get-tuple-element.746, pred[1024,512]{0,1:T(8,128)(4,1)S(1)} %and_and_fusion.5, bf16[1024,2,128]{2,0,1:T(8,128)(2,1)S(1)} %get-tuple-element.745, s32[]{:T(128)S(6)} %select_n.88, ...), kind=kOutput, calls=%fused_computation.12.clone.1 | convolution fusion | flops 544473088 | bytes 3671040 | tf_op jit(solution)/shard_map/while/body/eval_jaxpr/while/body/eval_jaxpr/hrk,khc->rhc/dot_general | solution.py:82
  80.2 4.6 %fusion.70 = f32[1024,2,128]{0,2,1:T(8,128)} fusion(f32[1024,2,128]{0,2,1:T(8,128)} %get-tuple-element.724, bf16[1024,2,128]{2,0,1:T(8,128)(2,1)} %get-tuple-element.746, pred[1024,512]{0,1:T(8,128)(4,1)S(1)} %and_and_fusion.5, bf16[1024,2,128]{2,0,1:T(8,128)(2,1)S(1)} %get-tuple-element.745, s32[]{:T(128)S(6)} %select_n.88, ...), kind=kOutput, calls=%fused_computation.12.clone.1 | convolution fusion | flops 544473088 | bytes 3671040 | tf_op jit(solution)/shard_map/while/body/eval_jaxpr/while/body/eval_jaxpr/hrk,khc->rhc/dot_general | solution.py:82
  90.2 2.4 %fusion.49 = bf16[1,1024,2,128]{3,1,2,0:T(8,128)(2,1)} fusion(f32[1024,2,128]{2,0,1:T(8,128)S(1)} %copy.38, bf16[1024,2,512]{2,0,1:T(8,128)(2,1)} %copy-done.2, f32[2,128]{1,0:T(2,128)S(1)} %copy-done.4, f32[1024,2]{0,1:T(2,128)S(1)} %add_rsqrt_fusion, f32[1024,2]{0,1:T(2,128)S(1)} %broadcast_multiply_fusion), kind=kLoop, calls=%fused_computation.63 | loop fusion | flops 1572864 | bytes 2114560 | tf_op jit(solution)/shard_map/broadcast_in_dim | solution.py:15
  93.8 11.9 %collective-permute-done.2 = bf16[1,1024,2,128]{3,1,2,0:T(8,128)(2,1)} collective-permute-done((bf16[1,1024,2,128]{3,1,2,0:T(8,128)(2,1)}, bf16[1,1024,2,128]{3,1,2,0:T(8,128)(2,1)}, u32[]{:S(2)}, u32[]{:S(2)}) %collective-permute-start.2) | collective-permute-done | bytes 524320 | tf_op jit(solution)/shard_map/ppermute | solution.py:17
  108.1 2.3 %collective-permute-start.3 = (bf16[2,1024,2,128]{3,1,2,0:T(8,128)(2,1)}, bf16[2,1024,2,128]{3,1,2,0:T(8,128)(2,1)}, u32[]{:S(2)}, u32[]{:S(2)}) collective-permute-start(bf16[2,1024,2,128]{3,1,2,0:T(8,128)(2,1)} %pad_maximum_fusion.1), channel_id=1, source_target_pairs={{0,2},{1,3},{2,0},{3,1},{4,6},{5,7},{6,4},{7,5},{8,10},{9,11},{10,... | collective-permute-start | bytes 3145736 | tf_op jit(solution)/shard_map/ppermute | solution.py:17
  112.4 4.1 %all-to-all-start = ((bf16[2,128,1024]{1,0,2:T(2,128)(2,1)}), bf16[2,128,1024]{1,0,2:T(2,128)(2,1)}, u32[]{:S(2)}, u32[]{:S(2)}) async-start(bf16[2,128,1024]{1,0,2:T(2,128)(2,1)} %copy.39), calls=%async_computation | async-start | bytes 1048576 | tf_op jit(solution)/shard_map/all_to_all | solution.py:113
  116.5 4.0 %convert_element_type.33 = f32[1024,1024]{1,0:T(8,128)} convert(bf16[1024,1024]{1,0:T(8,128)(2,1)} %param.12) | non-fusion elementwise | flops 1048576 | bytes 6291456 | tf_op jit(solution)/shard_map/convert_element_type | solution.py:42
  120.5 46.6 %all-to-all-done = bf16[2,128,1024]{1,0,2:T(2,128)(2,1)} async-done(((bf16[2,128,1024]{1,0,2:T(2,128)(2,1)}), bf16[2,128,1024]{1,0,2:T(2,128)(2,1)}, u32[]{:S(2)}, u32[]{:S(2)}) %all-to-all-start) | async-done | bytes 524320 | tf_op jit(solution)/shard_map/all_to_all | solution.py:113
  170.8 2.7 %fusion.48 = bf16[1024,256]{1,0:T(8,128)(2,1)} fusion(bf16[1024,8,128]{2,0,1:T(8,128)(2,1)S(1)} %bitcast.93, bf16[8,128,256]{2,1,0:T(8,128)(2,1)S(1)} %bitcast.94, f32[1024,1024]{1,0:T(8,128)} %convert_element_type.33, s32[]{:T(128)S(6)} %select_n.42), kind=kOutput, calls=%fused_computation.57 | convolution fusion | flops 537395200 | bytes 4194308 | tf_op jit(solution)/shard_map/rhc,hcd->rd/dot_general | solution.py:114
  (82 shorter events, 35.6 us)
Async XLA Ops:
  0.0 4.4 %copy-start = (bf16[1024,2,512]{2,1,0:T(2,128)(2,1)S(1)}, bf16[1024,2,512]{2,1,0:T(2,128)(2,1)}, u32[]{:S(2)}) copy-start(bf16[1024,2,512]{2,1,0:T(2,128)(2,1)} %param.15) | copy-start | bytes 6291460
  0.0 4.4 %copy-start.6 = (f32[1024]{0:T(1024)S(1)}, f32[1024]{0:T(1024)}, u32[]{:S(2)}) copy-start(f32[1024]{0:T(1024)} %param.14) | copy-start | bytes 12292
  0.0 4.4 %copy-start.1 = (bf16[1024,1024]{1,0:T(8,128)(2,1)S(1)}, bf16[1024,1024]{1,0:T(8,128)(2,1)}, u32[]{:S(2)}) copy-start(bf16[1024,1024]{1,0:T(8,128)(2,1)} %param.12) | copy-start | bytes 6291460
  7.9 1.4 copy-start.2
  9.2 1.5 copy-start.5
  24.0 10.1 %collective-permute-start = (bf16[1024,2,128]{2,0,1:T(8,128)(2,1)}, bf16[1024,2,128]{2,0,1:T(8,128)(2,1)S(1)}, u32[]{:S(2)}, u32[]{:S(2)}) collective-permute-start(bf16[1024,2,128]{2,0,1:T(8,128)(2,1)} %get-tuple-element.806), channel_id=1, source_target_pairs={{0,4},{4,8},{8,12},{12,16},{16,20},{20,24},{24,28},{1,5},{5,9},{9,... | collective-permute-start | bytes 1572872 | tf_op jit(solution)/shard_map/while/body/eval_jaxpr/ppermute | solution.py:31
  27.7 11.9 %collective-permute-start.1 = (bf16[1024,2,128]{0,2,1:T(8,128)(2,1)S(1)}, bf16[1024,2,128]{0,2,1:T(8,128)(2,1)}, u32[]{:S(2)}, u32[]{:S(2)}) collective-permute-start(bf16[1024,2,128]{0,2,1:T(8,128)(2,1)S(1)} %get-tuple-element.807), channel_id=1, source_target_pairs={{0,4},{4,8},{8,12},{12,16},{16,20},{20,24},{24,28},{1,5},{5,9},{9,... | collective-permute-start | bytes 1572872 | tf_op jit(solution)/shard_map/while/body/eval_jaxpr/ppermute | solution.py:31
  54.4 11.8 %collective-permute-start = (bf16[1024,2,128]{2,0,1:T(8,128)(2,1)}, bf16[1024,2,128]{2,0,1:T(8,128)(2,1)S(1)}, u32[]{:S(2)}, u32[]{:S(2)}) collective-permute-start(bf16[1024,2,128]{2,0,1:T(8,128)(2,1)} %get-tuple-element.806), channel_id=1, source_target_pairs={{0,4},{4,8},{8,12},{12,16},{16,20},{20,24},{24,28},{1,5},{5,9},{9,... | collective-permute-start | bytes 1572872 | tf_op jit(solution)/shard_map/while/body/eval_jaxpr/ppermute | solution.py:31
  59.8 11.9 %collective-permute-start.1 = (bf16[1024,2,128]{0,2,1:T(8,128)(2,1)S(1)}, bf16[1024,2,128]{0,2,1:T(8,128)(2,1)}, u32[]{:S(2)}, u32[]{:S(2)}) collective-permute-start(bf16[1024,2,128]{0,2,1:T(8,128)(2,1)S(1)} %get-tuple-element.807), channel_id=1, source_target_pairs={{0,4},{4,8},{8,12},{12,16},{16,20},{20,24},{24,28},{1,5},{5,9},{9,... | collective-permute-start | bytes 1572872 | tf_op jit(solution)/shard_map/while/body/eval_jaxpr/ppermute | solution.py:31
  86.6 3.6 %copy-start.4 = (f32[2,128]{1,0:T(2,128)S(1)}, f32[2,128]{1,0:T(2,128)}, u32[]{:S(2)}) copy-start(f32[2,128]{1,0:T(2,128)} %param.16) | copy-start | bytes 3076
  92.5 13.2 %collective-permute-start.2 = (bf16[1,1024,2,128]{3,1,2,0:T(8,128)(2,1)}, bf16[1,1024,2,128]{3,1,2,0:T(8,128)(2,1)}, u32[]{:S(2)}, u32[]{:S(2)}) collective-permute-start(bf16[1,1024,2,128]{3,1,2,0:T(8,128)(2,1)} %fusion.49), channel_id=1, source_target_pairs={{0,1},{1,0},{2,3},{3,2},{4,5},{5,4},{6,7},{7,6},{8,9},{9,8},{10,11... | collective-permute-start | bytes 1572872 | tf_op jit(solution)/shard_map/ppermute | solution.py:17
  108.1 61.0 %collective-permute-start.3 = (bf16[2,1024,2,128]{3,1,2,0:T(8,128)(2,1)}, bf16[2,1024,2,128]{3,1,2,0:T(8,128)(2,1)}, u32[]{:S(2)}, u32[]{:S(2)}) collective-permute-start(bf16[2,1024,2,128]{3,1,2,0:T(8,128)(2,1)} %pad_maximum_fusion.1), channel_id=1, source_target_pairs={{0,2},{1,3},{2,0},{3,1},{4,6},{5,7},{6,4},{7,5},{8,10},{9,11},{10,... | collective-permute-start | bytes 3145736 | tf_op jit(solution)/shard_map/ppermute | solution.py:17
  112.4 54.7 %all-to-all-start = ((bf16[2,128,1024]{1,0,2:T(2,128)(2,1)}), bf16[2,128,1024]{1,0,2:T(2,128)(2,1)}, u32[]{:S(2)}, u32[]{:S(2)}) async-start(bf16[2,128,1024]{1,0,2:T(2,128)(2,1)} %copy.39), calls=%async_computation | async-start | bytes 1048576 | tf_op jit(solution)/shard_map/all_to_all | solution.py:113
  169.0 1.8 %copy-start.3 = (bf16[2,128,4,256]{3,1,0,2:T(8,128)(2,1)S(1)}, bf16[2,128,4,256]{3,1,0,2:T(8,128)(2,1)}, u32[]{:S(2)}) copy-start(bf16[2,128,4,256]{3,1,0,2:T(8,128)(2,1)} %copy.40) | copy-start | bytes 1572868
